TPU v7x, 128 devices: a whole 4x4x4 slice. The times are simulated.
128 devices in a mesh: req: 16 (over y, x), seq: 4 (over z), hid: 2 (over core).
Axes of the slice: x: 4, y: 4, z: 4, core: 2. Of those that a mesh axis runs over, the one named last changes fastest.
Arguments:
- tokens: bfloat16 [65536, 2048], P(('req', 'seq')), may hold values from -6 to 6
- attention_gain: bfloat16 [2048], replicated, may hold values from 0.099609375 to 1.8984375
- project_weight: bfloat16 [2048, 2048], P(None, 'hid'), may hold values from -0.125 to 0.125
- conv_weight: bfloat16 [4, 2048], P(None, 'hid'), may hold values from -3 to 3
- decay_down: bfloat16 [2048, 16], replicated, may hold values from -0.125 to 0.125
- decay_up: bfloat16 [16, 512], P(None, 'hid'), may hold values from -1.5 to 1.5
- decay_bias: float32 [512], P('hid'), may hold values from -2 to 10
- output_gate: bfloat16 [2048, 1024], P(None, 'hid'), may hold values from -0.125 to 0.125
- head_gain: bfloat16 [512], replicated, may hold values from 0.099609375 to 1.8984375
- output_weight: bfloat16 [1024, 2048], P('hid'), may hold values from -0.1875 to 0.1875
- mixer_gain: bfloat16 [2048], replicated, may hold values from 0.099609375 to 1.8984375
- gate_weight: bfloat16 [2048, 2816], P('req', 'hid'), may hold values from -0.125 to 0.125
- up_weight: bfloat16 [2048, 2816], P('req', 'hid'), may hold values from -0.125 to 0.125
- down_weight: bfloat16 [2816, 2048], P('hid', 'req'), may hold values from -0.109375 to 0.109375
- prompt_pages: int32 [16, 16], P('req'), may hold values from 0 to 64, as said below
- prompt_start: int32 [16, 16], P('req'), may hold values from 0 to 63, as said below
Outputs:
- hidden_out: bfloat16 [65536, 2048], P(('req', 'seq', 'hid'))
- page_states: bfloat16 [1024, 2, 256, 512], P(('req', 'seq'), 'hid')
- conv_edges: bfloat16 [1024, 3, 2048], P(('req', 'seq'), None, 'hid')
Inputs may be any that keep to these rules, and one draw needn't show every extreme that they name: `prompt_pages`: row r lists the page counts of the prompts of group r; 0 marks an unused slot; in every draw some group holds one prompt of all its 64 pages. `prompt_start`: the slots of a row that are used cover pages in increasing order without intersection and end by page 64; pages between prompts belong to none; an unused slot starts at page 64 - 1, and every draw has one.
All inputs are finite; a program needn't handle non-finite values.
Results may differ from a plain program's by a relative error of at most 0.014.
Values may be sent and summed in bfloat16 or wider, within the bound.
A program may use at most 192 MiB of HBM per device.

v0:
```python
import jax
import jax.numpy as jnp
from jax import lax
from jax.sharding import PartitionSpec as P

HK = 256
HV = 512
KCONV = 4
PAGE = 64
CONVW = 1024
EPSILON = 1e-06
TOP_PRECISION = lax.Precision.HIGHEST


def shifted(value, axis, steps):
    count = lax.axis_size(axis)
    first, last = (max(0, -steps), min(count, count - steps))
    return lax.ppermute(value, axis, [(source, source + steps) for source in range(first, last)])


def prefix_2(array, axis, join, neutral):
    place = lax.axis_index(axis)
    gathered = jax.tree.map(
        lambda a, kind: lax.all_gather(a.astype(kind), axis), array, (jnp.bfloat16, jnp.bfloat16)
    )
    state = jax.tree.map(lambda a, e: jnp.zeros_like(a) + jnp.asarray(e, a.dtype), array, neutral)

    def one(lap, state):
        return join(
            state,
            jax.tree.map(
                lambda a, own: lax.dynamic_index_in_dim(a, lap, 0, False).astype(own.dtype),
                gathered,
                array,
            ),
        )

    return lax.fori_loop(0, place, one, state)


def rms_scaled(values, scale_gain):
    values = values.astype(jnp.float32)
    return (
        values
        * lax.rsqrt(jnp.mean(values * values, axis=-1, keepdims=True) + EPSILON)
        * scale_gain.astype(jnp.float32)
    )


def page_segments(page_counts, starts, total_pages):
    position = jnp.arange(total_pages, dtype=jnp.int32)
    inside = (position[None, :] >= starts[:, None]) & (
        position[None, :] < starts[:, None] + page_counts[:, None]
    )
    labels = jnp.arange(1, page_counts.shape[0] + 1, dtype=jnp.int32)
    segment = jnp.sum(jnp.where(inside, labels[:, None], 0), axis=0) - 1
    earlier = jnp.concatenate([jnp.full((1,), -1, jnp.int32), segment[:-1]])
    return ((segment == earlier) & (segment >= 0)).astype(jnp.float32)


def short_conv(by_page, before, carried, conv_taps):
    kept_rows = before.astype(jnp.float32) * carried[:, None, None]
    widened = jnp.concatenate([kept_rows, by_page.astype(jnp.float32)], axis=1)
    tap_count = conv_taps.shape[0]
    length = by_page.shape[1]
    result = jnp.zeros(by_page.shape, jnp.float32)
    for offset in range(tap_count):
        result = (
            result
            + conv_taps[offset].astype(jnp.float32)
            * widened[:, tap_count - 1 - offset : tap_count - 1 - offset + length]
        )
    return result


def split_features(mixed_rows, key_width):
    query_rows = jax.nn.silu(mixed_rows[..., :key_width])
    key_rows = jax.nn.silu(mixed_rows[..., key_width : 2 * key_width]) * key_width ** (-0.5)
    value_matrix = mixed_rows[..., 2 * key_width :]
    return (
        query_rows.transpose(0, 2, 1, 3),
        key_rows.transpose(0, 2, 1, 3),
        value_matrix.transpose(0, 2, 1, 3),
    )


def page_block(query_rows, key_rows, value_matrix, decay_sum, carried):
    length = query_rows.shape[2]
    page_count = query_rows.shape[0]
    raised_rows = query_rows * jnp.exp(decay_sum)
    lowered = key_rows * jnp.exp(-decay_sum)
    scores = jnp.einsum("phik,phjk->phij", raised_rows, lowered, precision=TOP_PRECISION)
    rows_index = jnp.arange(length)
    causal = rows_index[:, None] >= rows_index[None, :]
    scores = jnp.where(causal[None, None], scores, 0.0)
    layer_output = jnp.einsum("phij,phjv->phiv", scores, value_matrix, precision=TOP_PRECISION)
    closing_sum = decay_sum[:, :, -1, :]
    weighted_rows = key_rows * jnp.exp(closing_sum[:, :, None, :] - decay_sum)
    page_terms = jnp.einsum("phte,phtb->pheb", weighted_rows, value_matrix, precision=TOP_PRECISION)
    through = jnp.cumsum(closing_sum, axis=0)
    resets = jnp.cumsum(1.0 - carried)
    pages = jnp.arange(page_count)
    valid = (pages[:, None] >= pages[None, :]) & (resets[:, None] == resets[None, :])
    spread = through[:, None] - through[None, :]
    spread = jnp.where(valid[:, :, None, None], spread, 0.0)
    weights = jnp.where(valid[:, :, None, None], jnp.exp(spread), 0.0)
    memories = jnp.einsum("pqhe,qheb->pheb", weights, page_terms, precision=TOP_PRECISION)
    previous = jnp.concatenate([jnp.zeros_like(memories[:1]), memories[:-1]], axis=0)
    previous = previous * carried[:, None, None, None]
    layer_output = layer_output + jnp.einsum(
        "phik,phkv->phiv", raised_rows, previous, precision=TOP_PRECISION
    )
    return (memories[-1], layer_output, memories)


def on_device(
    tokens,
    attention_gain,
    project_weight,
    conv_weight,
    decay_down,
    decay_up,
    decay_bias,
    output_gate,
    head_gain,
    output_weight,
    mixer_gain,
    gate_weight,
    up_weight,
    down_weight,
    prompt_pages,
    prompt_start,
):
    token_count = tokens.shape[0]
    page_count = token_count // PAGE
    local_heads = project_weight.shape[1] // CONVW
    rim_rows = KCONV - 1
    seq_index = lax.axis_index("seq")
    group_pages = page_count * lax.axis_size("seq")
    page_flags = page_segments(prompt_pages[0], prompt_start[0], group_pages)
    carried = lax.dynamic_slice_in_dim(page_flags, seq_index * page_count, page_count)
    normed = rms_scaled(tokens, attention_gain).astype(jnp.bfloat16)
    projected = jnp.dot(normed, project_weight, preferred_element_type=jnp.float32).astype(
        jnp.bfloat16
    )
    by_page = projected.reshape(page_count, PAGE, local_heads * CONVW)
    incoming = shifted(by_page[-1, PAGE - rim_rows :], "seq", 1)
    before = jnp.concatenate([incoming[None], by_page[:-1, PAGE - rim_rows :]], axis=0)
    mixed_rows = short_conv(by_page, before, carried, conv_weight).reshape(
        page_count, PAGE, local_heads, CONVW
    )
    query_rows, key_rows, value_matrix = split_features(mixed_rows, HK)
    lowrank = jnp.dot(normed, decay_down, preferred_element_type=jnp.float32).astype(jnp.bfloat16)
    decay_log = (
        jax.nn.log_sigmoid(
            jnp.dot(lowrank, decay_up, preferred_element_type=jnp.float32) + decay_bias
        )
        / 16.0
    )
    decay_log = decay_log.reshape(page_count, PAGE, local_heads, HK).transpose(0, 2, 1, 3)
    decay_sum = jnp.cumsum(decay_log, axis=2)
    local_memory, outputs, memories = page_block(
        query_rows, key_rows, value_matrix, decay_sum, carried
    )
    totals = decay_sum[:, :, -1, :]
    through = jnp.cumsum(totals, axis=0)
    alive_mask = jnp.cumprod(carried)
    block_decay = alive_mask[-1] * jnp.exp(through[-1])

    def compose(earlier, latter):
        return (earlier[0] * latter[0], latter[0][..., None] * earlier[1] + latter[1])

    prefix = prefix_2(
        (block_decay, local_memory),
        "seq",
        compose,
        (jnp.ones_like(block_decay), jnp.zeros_like(local_memory)),
    )
    incoming_state = prefix[1]
    before_sum = through - totals
    extent_factor = alive_mask[:, None, None, None] * jnp.exp(decay_sum + before_sum[:, :, None, :])
    outputs = outputs + jnp.einsum(
        "dlof,lfg->dlog", query_rows * extent_factor, incoming_state, precision=TOP_PRECISION
    )
    memories = (
        memories + (alive_mask[:, None, None] * jnp.exp(through))[..., None] * incoming_state[None]
    )
    attended = outputs.transpose(0, 2, 1, 3).reshape(token_count, local_heads, HV)
    normed_heads = rms_scaled(attended, head_gain)
    opening = jax.nn.silu(jnp.dot(normed, output_gate, preferred_element_type=jnp.float32)).reshape(
        token_count, local_heads, HV
    )
    gated_rows = (
        (normed_heads * opening).astype(jnp.bfloat16).reshape(token_count, local_heads * HV)
    )
    partial_value = jnp.dot(gated_rows, output_weight, preferred_element_type=jnp.float32)
    half_rows = token_count // lax.axis_size("hid")
    row_start = lax.axis_index("hid") * half_rows
    mixed_sum = lax.psum(partial_value.astype(jnp.bfloat16), "hid").astype(jnp.float32)
    residual = (tokens.astype(jnp.float32) + mixed_sum).astype(jnp.bfloat16)
    feed_in = rms_scaled(residual, mixer_gain).astype(jnp.bfloat16)
    own_residual = lax.dynamic_slice_in_dim(residual, row_start, half_rows, 0)

    def widen(weight_rows):
        return jnp.dot(feed_in, weight_rows, preferred_element_type=jnp.float32)

    gate_part = widen(lax.all_gather(gate_weight, "req", axis=0, tiled=True))
    up_part = widen(lax.all_gather(up_weight, "req", axis=0, tiled=True))
    hidden = (jax.nn.silu(gate_part) * up_part).astype(jnp.bfloat16)
    partials = jnp.dot(
        hidden,
        lax.all_gather(down_weight, "req", axis=1, tiled=True),
        preferred_element_type=jnp.float32,
    )
    feed_sum = lax.psum_scatter(
        partials.astype(jnp.bfloat16), "hid", scatter_dimension=0, tiled=True
    ).astype(jnp.float32)
    result = (own_residual.astype(jnp.float32) + feed_sum).astype(jnp.bfloat16)
    return (result, memories.astype(jnp.bfloat16), by_page[:, PAGE - rim_rows :])


def solution(mesh):
    return jax.shard_map(
        on_device,
        mesh=mesh,
        in_specs=(
            P(("req", "seq"), None),
            P(),
            P(None, "hid"),
            P(None, "hid"),
            P(),
            P(None, "hid"),
            P("hid"),
            P(None, "hid"),
            P(),
            P("hid", None),
            P(),
            P("req", "hid"),
            P("req", "hid"),
            P("hid", "req"),
            P("req", None),
            P("req", None),
        ),
        out_specs=(
            P(("req", "seq", "hid"), None),
            P(("req", "seq"), "hid", None, None),
            P(("req", "seq"), None, "hid"),
        ),
        check_vma=False,
    )
```

profile of v0, /device:TPU:1, one launch (start us, length us, event | category | flops | bytes accessed | tf_op | source)
XLA Modules:
  0.0 364.4 jit_solution(5683534701682440027)
XLA Ops:
  11.7 7.3 %convolution_convert_fusion.2 = bf16[1024,1024]{1,0:T(8,128)(2,1)S(1)} fusion(bf16[2048,1024]{1,0:T(8,128)(2,1)} %param.20, bf16[1024,2048]{1,0:T(8,128)(2,1)S(1)} %copy-done.6, f32[2048]{0:T(1024)S(1)} %convert_element_type.149, f32[1024]{0:T(1024)S(1)} %add_rsqrt_fusion.2), kind=kOutput, calls=%fused_computation.53 | convolution fusion | flops 4304404480 | bytes 10498048 | tf_op jit(solution)/shard_map/dot_general | solution.py:143
  20.3 4.4 %collective-permute-start = (bf16[3,1024]{1,0:T(4,128)(2,1)S(1)}, bf16[3,1024]{1,0:T(4,128)(2,1)S(1)}, u32[]{:S(2)}, u32[]{:S(2)}) collective-permute-start(bf16[3,1024]{1,0:T(4,128)(2,1)S(1)} %slice_bitcast_fusion.5), channel_id=1, source_target_pairs={{0,2},{2,4},{4,6},{1,3},{3,5},{5,7},{8,10},{10,12},{12,14},{9,11},... | collective-permute-start | bytes 18440 | tf_op jit(solution)/shard_map/ppermute | solution.py:18
  24.9 5.2 %fusion.37 = f32[1024,256]{1,0:T(8,128)} fusion(bf16[16,256]{1,0:T(8,128)(2,1)S(1)} %copy-done.15, bf16[2048,16]{0,1:T(8,128)(2,1)S(1)} %copy-done.14, f32[256]{0:T(256)S(1)} %copy-done.16, bf16[1024,2048]{1,0:T(8,128)(2,1)} %param.18, f32[2048]{0:T(1024)S(1)} %convert_element_type.149, f32[1024]{0:T(1024)S(1)} %add_rsqrt_fusion.2), kind=kOutput, calls=%fused_computation.60 | convolution fusion | flops 86523904 | bytes 5329920 | tf_op jit(solution)/shard_map/dot_general | solution.py:156
  34.8 4.1 %convert_element_type.152 = f32[16,64,1024]{2,1,0:T(8,128)} convert(bf16[16,64,1024]{2,1,0:T(8,128)(2,1)} %bitcast.138) | non-fusion elementwise | flops 1048576 | bytes 6291456 | tf_op jit(solution)/shard_map/convert_element_type | solution.py:63
  39.1 6.9 %all_gather.17 = bf16[4,1,256]{2,1,0:T(2,128)(2,1)S(1)} all-gather(bf16[1,1,256]{2,1,0:T(2,128)(2,1)S(1)} %fusion.71), channel_id=1, replica_groups=mesh['req'=16,'seq'=4,'hid'=2] {'seq'}, dimensions={0}, use_global_device_ids=true | all-gather | bytes 2560 | tf_op jit(solution)/shard_map/all_gather | solution.py:24
  46.1 7.6 %fusion.15 = f32[16,64,1,1024]{3,1,0,2:T(8,128)S(1)} fusion(f32[16,64,1024]{2,1,0:T(8,128)} %convert_element_type.152, f32[16,3,1024]{2,1,0:T(4,128)S(1)} %convert_multiply_fusion.4, f32[1024]{0:T(1024)S(1)} %bitcast.145, f32[1024]{0:T(1024)S(1)} %bitcast.146, f32[1024]{0:T(1024)S(1)} %bitcast.144, f32[1024]{0:T(1024)S(1)} %bitcast.143), kind=kLoop, calls=%fused_computation.29 | loop fusion | flops 10485760 | bytes 8601600 | tf_op jit(solution)/shard_map/reshape | solution.py:149
  53.7 7.4 %fusion.30 = f32[16,256,512]{2,1,0:T(8,128)S(1)} fusion(f32[16,64,1,1024]{3,1,0,2:T(8,128)S(1)} %fusion.15, f32[16,1,64,256]{3,0,1,2:T(8,128)S(1)} %fusion.48, f32[16,256]{1,0:T(8,128)S(1)} %get-tuple-element.85), kind=kOutput, calls=%fused_computation.51 | convolution fusion | flops 1612447744 | bytes 12599296 | tf_op jit(solution)/shard_map/phte,phtb->pheb/dot_general | solution.py:99
  61.1 13.6 %fusion.20 = f32[16,1,256,512]{3,0,2,1:T(8,128)S(1)} fusion(f32[16,256,512]{2,1,0:T(8,128)S(1)} %fusion.30, f32[16,256]{0,1:T(8,128)S(1)} %bitcast.140, pred[16,16]{1,0:T(8,128)(4,1)S(1)} %fusion.69), kind=kOutput, calls=%fused_computation.38 | convolution fusion | flops 402849792 | bytes 16793856 | tf_op jit(solution)/shard_map/pqhe,qheb->pheb/dot_general | solution.py:107
  79.5 4.2 %convolution_select_fusion = f32[16,64,64]{2,1,0:T(8,128)S(1)} fusion(f32[16,1,64,256]{3,0,1,2:T(8,128)S(1)} %fusion.48, pred[64,64]{1,0:T(8,128)(4,1)S(1)} %iota_compare_fusion, f32[16,64,1,1024]{3,1,0,2:T(8,128)} %copy-done.3), kind=kOutput, calls=%fused_computation.56 | convolution fusion | flops 204537856 | bytes 4464640 | tf_op jit(solution)/shard_map/phik,phjk->phij/dot_general | solution.py:92
  86.9 5.3 %multiply_bitcast_fusion = f32[16,256,512]{2,0,1:T(8,128)S(1)} fusion(f32[15,1,256,512]{3,0,2,1:T(8,128)} %bitcast.134, f32[16]{0:T(128)S(1)} %get-tuple-element.83), kind=kLoop, calls=%fused_computation.19 | loop fusion | flops 2097152 | bytes 16252992 | tf_op jit(solution)/shard_map/reshape.33
  92.3 13.1 %fusion.7 = f32[16,64,512]{2,1,0:T(8,128)} fusion(f32[16,256,512]{2,0,1:T(8,128)S(1)} %multiply_bitcast_fusion, f32[16,1,64,256]{3,0,1,2:T(8,128)S(1)} %fusion.48, f32[16,64,1,1024]{3,1,0,2:T(8,128)} %copy-done.3), kind=kOutput, calls=%fused_computation.14 | convolution fusion | flops 1611923456 | bytes 12582912 | tf_op jit(solution)/shard_map/phik,phkv->phiv/dot_general | solution.py:110
  105.5 6.8 %multiply_reduce_fusion = (f32[16,64]{1,0:T(8,128)S(1)}, f32[16,1,64,512]{3,2,0,1:T(8,128)}) fusion(f32[16,1,64,256]{3,0,1,2:T(8,128)} %copy-done.5, f32[16,256]{1,0:T(8,128)S(1)} %get-tuple-element.84, f32[16]{0:T(128)S(1)} %reduce.3, f32[16,64,1,1024]{3,1,0,2:T(8,128)} %copy-done.3, f32[1,256,512]{2,1,0:T(8,128)S(1)} %get-tuple-element.47, ...), kind=kOutput, calls=%fused_computation.46 | convolution fusion | flops 1614543872 | bytes 8933440 | tf_op jit(solution)/shard_map/dlof,lfg->dlog/dot_general | solution.py:182
  112.4 6.2 %fusion.25 = bf16[1024,512]{1,0:T(8,128)(2,1)S(1)} fusion(f32[16,1,64,512]{3,2,0,1:T(8,128)} %get-tuple-element.91, f32[512]{0:T(512)S(1)} %convert_element_type.163, f32[1024]{0:T(1024)S(1)} %rsqrt.29, bf16[2048,512]{1,0:T(8,128)(2,1)} %param.25, bf16[1024,2048]{1,0:T(8,128)(2,1)} %param.18, f32[2048]{0:T(1024)S(1)} %convert_element_type.149, ...), kind=kOutput, calls=%fused_computation.45 | convolution fusion | flops 2160066560 | bytes 9455616 | tf_op jit(solution)/shard_map/dot_general | solution.py:190
  118.5 4.4 %convolution_convert_fusion.1 = bf16[1024,2048]{1,0:T(8,128)(2,1)} fusion(bf16[1024,512]{1,0:T(8,128)(2,1)S(1)} %fusion.25, bf16[512,2048]{1,0:T(8,128)(2,1)S(1)} %copy-done), kind=kOutput, calls=%fused_computation.37 | convolution fusion | flops 2149580800 | bytes 7340032 | tf_op jit(solution)/shard_map/dot_general | solution.py:196
  125.0 37.7 %all-reduce.3.cloned.1.call-done = bf16[1024,2048]{1,0:T(8,128)(2,1)} async-done(((bf16[1024,2048]{1,0:T(8,128)(2,1)}), bf16[1024,2048]{1,0:T(8,128)(2,1)}) %all-reduce.3.cloned.1.call-update) | async-done | bytes 4194320 | tf_op jit(solution)/shard_map/psum | solution.py:199
  162.7 7.7 %fusion = (f32[1024]{0:T(1024)S(1)}, bf16[1024,2048]{1,0:T(8,128)(2,1)}) fusion(bf16[1024,2048]{1,0:T(8,128)(2,1)} %all-reduce.3.cloned.1.call-done, bf16[1024,2048]{1,0:T(8,128)(2,1)} %param.18), kind=kLoop, calls=%fused_computation.7 | loop fusion | flops 14679040 | bytes 12587008 | tf_op jit(solution)/shard_map/reduce_sum | solution.py:45
  170.4 19.1 %all-gather.7.cloned.1.call-done = bf16[2048,1408]{1,0:T(8,128)(2,1)} async-done(((bf16[128,1408]{1,0:T(8,128)(2,1)}), bf16[2048,1408]{1,0:T(8,128)(2,1)}) %all-gather.7.cloned.1.call-update) | async-done | bytes 5767184 | tf_op jit(solution)/shard_map/all_gather | solution.py:207
  189.4 12.0 %fusion.34 = f32[1024,1408]{1,0:T(8,128)} fusion(bf16[2048,1408]{1,0:T(8,128)(2,1)} %all-gather.7.cloned.1.call-done, bf16[1024,2048]{1,0:T(8,128)(2,1)} %get-tuple-element.81, f32[2048]{0:T(1024)S(1)} %convert_element_type.170, f32[1024]{0:T(1024)S(1)} %add_rsqrt_fusion.1), kind=kOutput, calls=%fused_computation.57 | convolution fusion | flops 5913968640 | bytes 15740928 | tf_op jit(solution)/shard_map/dot_general | solution.py:205
  201.4 53.5 %all-gather.11.cloned.1.call-done = bf16[1408,2048]{1,0:T(8,128)(2,1)} async-done(((bf16[1408,128]{1,0:T(8,128)(2,1)}), bf16[1408,2048]{1,0:T(8,128)(2,1)}) %all-gather.11.cloned.1.call-update) | async-done | bytes 5767184 | tf_op jit(solution)/shard_map/all_gather | solution.py:212
  254.9 61.3 %all-gather.9.cloned.1.call-done = bf16[2048,1408]{1,0:T(8,128)(2,1)} async-done(((bf16[128,1408]{1,0:T(8,128)(2,1)}), bf16[2048,1408]{1,0:T(8,128)(2,1)}) %all-gather.9.cloned.1.call-update) | async-done | bytes 5767184 | tf_op jit(solution)/shard_map/all_gather | solution.py:208
  316.1 20.9 %convolution_convert_fusion = bf16[1024,2048]{1,0:T(8,128)(2,1)} fusion(bf16[1408,2048]{1,0:T(8,128)(2,1)} %all-gather.11.cloned.1.call-done, f32[1024,1408]{1,0:T(8,128)} %fusion.34, bf16[2048,1408]{1,0:T(8,128)(2,1)} %all-gather.9.cloned.1.call-done, bf16[1024,2048]{1,0:T(8,128)(2,1)} %get-tuple-element.81, f32[2048]{0:T(1024)S(1)} %convert_element_type.170, ...), kind=kOutput, calls=%fused_computation.36 | convolution fusion | flops 11830296576 | bytes 25702400 | tf_op jit(solution)/shard_map/dot_general | solution.py:210
  342.9 4.4 %copy.71 = bf16[16,1,256,512]{3,2,1,0:T(8,128)(2,1)} copy(bf16[16,1,256,512]{3,0,2,1:T(8,128)(2,1)S(1)} %add_convert_fusion) | data formatting | bytes 8388608
  347.3 4.8 %reduce-scatter.2.cloned.1.call-done = bf16[512,2048]{1,0:T(8,128)(2,1)} async-done(((bf16[1024,2048]{1,0:T(8,128)(2,1)}), bf16[512,2048]{1,0:T(8,128)(2,1)}) %reduce-scatter.2.cloned.1.call-update) | async-done | bytes 2097168 | tf_op jit(solution)/shard_map/reduce_scatter | solution.py:215
  352.1 4.4 %add_convert_fusion.1 = bf16[512,2048]{1,0:T(8,128)(2,1)} fusion(bf16[512,2048]{1,0:T(8,128)(2,1)} %reduce-scatter.2.cloned.1.call-done, bf16[1024,2048]{1,0:T(8,128)(2,1)} %get-tuple-element.81, s32[]{:T(128)S(6)} %select_n.46), kind=kLoop, calls=%fused_computation.35 | loop fusion | flops 4194304 | bytes 6291460 | tf_op jit(solution)/shard_map/convert_element_type | solution.py:218
  (90 shorter events, 26.0 us)
Async XLA Ops:
  8.0 110.5 %copy-start = (bf16[512,2048]{1,0:T(8,128)(2,1)S(1)}, bf16[512,2048]{1,0:T(8,128)(2,1)}, u32[]{:S(2)}) copy-start(bf16[512,2048]{1,0:T(8,128)(2,1)} %param.27) | copy-start | bytes 6291460
  8.0 3.3 copy-start.9
  8.0 97.4 %all-gather.5.cloned.1.call-start = ((), (), s32[]{:S(2)}) async-start(), calls=%async_computation.1 | async-start | bytes 1310720 | tf_op jit(solution)/shard_map/all_gather | solution.py:24
  8.1 3.6 copy-start.6
  11.6 13.0 %copy-start.11 = (s32[1,16]{1,0:T(1,128)S(1)}, s32[1,16]{1,0:T(1,128)}, u32[]{:S(2)}) copy-start(s32[1,16]{1,0:T(1,128)} %param.33) | copy-start | bytes 196
  11.6 13.0 %copy-start.13 = (s32[1,16]{1,0:T(1,128)S(1)}, s32[1,16]{1,0:T(1,128)}, u32[]{:S(2)}) copy-start(s32[1,16]{1,0:T(1,128)} %param.32) | copy-start | bytes 196
  11.6 13.2 %copy-start.8 = (bf16[4,1024]{1,0:T(4,128)(2,1)S(1)}, bf16[4,1024]{1,0:T(4,128)(2,1)}, u32[]{:S(2)}) copy-start(bf16[4,1024]{1,0:T(4,128)(2,1)} %param.21) | copy-start | bytes 24580
  11.6 13.2 %copy-start.14 = (bf16[2048,16]{0,1:T(8,128)(2,1)S(1)}, bf16[2048,16]{0,1:T(8,128)(2,1)}, u32[]{:S(2)}) copy-start(bf16[2048,16]{0,1:T(8,128)(2,1)} %param.22) | copy-start | bytes 196612
  11.6 13.2 %copy-start.15 = (bf16[16,256]{1,0:T(8,128)(2,1)S(1)}, bf16[16,256]{1,0:T(8,128)(2,1)}, u32[]{:S(2)}) copy-start(bf16[16,256]{1,0:T(8,128)(2,1)} %param.23) | copy-start | bytes 24580
  11.7 13.2 %copy-start.16 = (f32[256]{0:T(256)S(1)}, f32[256]{0:T(256)}, u32[]{:S(2)}) copy-start(f32[256]{0:T(256)} %param.24) | copy-start | bytes 3076
  18.9 1.3 copy-start.7
  20.3 25.7 %collective-permute-start = (bf16[3,1024]{1,0:T(4,128)(2,1)S(1)}, bf16[3,1024]{1,0:T(4,128)(2,1)S(1)}, u32[]{:S(2)}, u32[]{:S(2)}) collective-permute-start(bf16[3,1024]{1,0:T(4,128)(2,1)S(1)} %slice_bitcast_fusion.5), channel_id=1, source_target_pairs={{0,2},{2,4},{4,6},{1,3},{3,5},{5,7},{8,10},{10,12},{12,14},{9,11},... | collective-permute-start | bytes 18440 | tf_op jit(solution)/shard_map/ppermute | solution.py:18
  30.0 9.0 %copy-start.12 = (bf16[512]{0:T(512)(128)(2,1)S(1)}, bf16[512]{0:T(512)(128)(2,1)}, u32[]{:S(2)}) copy-start(bf16[512]{0:T(512)(128)(2,1)} %param.26) | copy-start | bytes 3076
  31.9 60.4 %copy-start.5 = (f32[16,1,64,256]{3,0,1,2:T(8,128)}, f32[16,1,64,256]{3,0,1,2:T(8,128)S(1)}, u32[]{:S(2)}) copy-start(f32[16,1,64,256]{3,0,1,2:T(8,128)S(1)} %fusion.48) | copy-start | bytes 3145732
  53.7 7.4 %copy-start.3 = (f32[16,64,1,1024]{3,1,0,2:T(8,128)}, f32[16,64,1,1024]{3,1,0,2:T(8,128)S(1)}, u32[]{:S(2)}) copy-start(f32[16,64,1,1024]{3,1,0,2:T(8,128)S(1)} %fusion.15) | copy-start | bytes 12582916
  74.7 3.2 copy-start.2
  79.3 83.3 %all-reduce.3.cloned.1.call-start = ((), (), s32[]{:S(2)}) async-start(), calls=%async_computation.2 | async-start | bytes 8388608 | tf_op jit(solution)/shard_map/psum | solution.py:199
  79.5 4.2 %copy-start.4 = (f32[16,64,1,1024]{3,1,0,2:T(8,128)S(1)}, f32[16,64,1,1024]{3,1,0,2:T(8,128)}, u32[]{:S(2)}) copy-start(f32[16,64,1,1024]{3,1,0,2:T(8,128)} %copy-done.3) | copy-start | bytes 12582916
  122.9 2.1 copy-start.10
  122.9 66.5 %all-gather.7.cloned.1.call-start = ((), (), s32[]{:S(2)}) async-start(), calls=%async_computation.3 | async-start | bytes 6127616 | tf_op jit(solution)/shard_map/all_gather | solution.py:207
  123.5 131.4 %all-gather.11.cloned.1.call-start = ((), (), s32[]{:S(2)}) async-start(), calls=%async_computation.5 | async-start | bytes 6127616 | tf_op jit(solution)/shard_map/all_gather | solution.py:212
  124.1 192.1 %all-gather.9.cloned.1.call-start = ((), (), s32[]{:S(2)}) async-start(), calls=%async_computation.4 | async-start | bytes 6127616 | tf_op jit(solution)/shard_map/all_gather | solution.py:208
  124.7 227.5 %reduce-scatter.2.cloned.1.call-start = ((), (), s32[]{:S(2)}) async-start(), calls=%async_computation.6 | async-start | bytes 6291456 | tf_op jit(solution)/shard_map/reduce_scatter | solution.py:215
  342.9 13.7 %copy-start.1 = (bf16[512,2048]{1,0:T(8,128)(2,1)S(1)}, bf16[512,2048]{1,0:T(8,128)(2,1)}, u32[]{:S(2)}) copy-start(bf16[512,2048]{1,0:T(8,128)(2,1)} %param.27) | copy-start | bytes 6291460
Sparse Core Ops, SparseCore 0:
  79.4 24.9 all-gather.4
  123.0 39.5 all-reduce.2
  337.2 14.9 reduce-scatter.1
Sparse Core Ops, SparseCore 1:
  125.7 63.6 all-gather.6
  191.6 63.2 all-gather.10
  257.1 59.0 all-gather.8
where the time goes:
time: 371 us; the launch traced here: 364 us
  waiting for transfers between devices  178 us (48%)
  matrix products  104 us (28%)
  other arithmetic  39.8 us (11%)
  between operations  16.3 us (4%)
  local copies, waits for them, and re-layouts  14.4 us (4%)
  blocking collectives  6.9 us (2%)
  starting transfers between devices  5.04 us (1%)
    all_gather x1, waiting for transfers between devices, on_device(): up_part = widen(lax.all_gather(up_weight, 'req', axis=0, tiled=True))  61.3 us
    all_gather x1, waiting for transfers between devices, on_device(): lax.all_gather(down_weight, 'req', axis=1, tiled=True)  53.5 us
    psum x1, waiting for transfers between devices, on_device(): lax.psum(partial_value.astype(jnp.bfloat16), 'hid').astype(jnp.float32)  37.7 us
    dot_general x1, matrix products, on_device(): jnp.dot(hidden, lax.all_gather(down_weight, 'req', axis=1, tiled=True), p...  20.9 us
    all_gather x1, waiting for transfers between devices, on_device(): gate_part = widen(lax.all_gather(gate_weight, 'req', axis=0, tiled=True))  19.1 us
    dot_general x1, matrix products, page_block(): jnp.einsum('pqhe,qheb->pheb', weights, page_terms, precision=TOP_PRECISION)  13.6 us
    dot_general x1, matrix products, page_block(): jnp.einsum('phik,phkv->phiv', raised_rows, previous, precision=TOP_PRECIS...  13.1 us
    dot_general x1, matrix products, widen(): return jnp.dot(feed_in, weight_rows, preferred_element_type=jnp.float32)  12 us
  transfers between devices with their start and end apart: 7, of which 5 were waited for; matrix products, arithmetic and copies ran while one was open for 19% of the time, Pallas kernels for 0%

commit v1 on v0

--- a/solution.py
+++ b/solution.py
@@ -2,6 +2,7 @@
 import jax.numpy as jnp
 from jax import lax
 from jax.sharding import PartitionSpec as P
+from jax.lax import all_gather
 
 HK = 256
 HV = 512
@@ -196,7 +197,9 @@
     partial_value = jnp.dot(gated_rows, output_weight, preferred_element_type=jnp.float32)
     half_rows = token_count // lax.axis_size("hid")
     row_start = lax.axis_index("hid") * half_rows
-    mixed_sum = lax.psum(partial_value.astype(jnp.bfloat16), "hid").astype(jnp.float32)
+    mixed_sum = jnp.sum(all_gather(partial_value.astype(jnp.bfloat16), "hid"), axis=0).astype(
+        jnp.float32
+    )
     residual = (tokens.astype(jnp.float32) + mixed_sum).astype(jnp.bfloat16)
     feed_in = rms_scaled(residual, mixer_gain).astype(jnp.bfloat16)
     own_residual = lax.dynamic_slice_in_dim(residual, row_start, half_rows, 0)

time: 371 us -> 393 us (1.059)
  waiting for transfers between devices: 178 us -> 193 us
  other arithmetic: 39.8 us -> 48.4 us
    psum x1 -> x0, waiting for transfers between devices: 37.7 us -> none  [on_device(): lax.psum(partial_value.astype(jnp.bfloat16), 'hid').astype(jnp.float32)]
    all_gather x1, waiting for transfers between devices: 19.1 us -> 45.5 us  [on_device(): gate_part = widen(lax.all_gather(gate_weight, 'req', axis=0, tiled=True))]
    all_gather x0 -> x1, waiting for transfers between devices: none -> 26.1 us  [on_device(): all_gather(partial_value.astype(jnp.bfloat16), 'hid')]
    all_gather x1, waiting for transfers between devices: 61.3 us -> 48.5 us  [on_device(): up_part = widen(lax.all_gather(up_weight, 'req', axis=0, tiled=True))]
    all_gather x1, waiting for transfers between devices: 53.5 us -> 65.9 us  [on_device(): lax.all_gather(down_weight, 'req', axis=1, tiled=True)]
    reduce_sum x0 -> x1, other arithmetic: none -> 8.78 us  [on_device(): jnp.sum(all_gather(partial_value.astype(jnp.bfloat16), 'hid'), axis=0)]
  transfers between devices with their start and end apart: 7 -> 7, of which waited for: 5 -> 5; matrix products, arithmetic and copies ran while one was open for 19% -> 20% of each run, Pallas kernels for 0% -> 0%
where the time goes in v1:
time: 393 us; the launch traced here: 387 us
  waiting for transfers between devices  193 us (49%)
  matrix products  104 us (26%)
  other arithmetic  48.4 us (12%)
  between operations  14.7 us (4%)
  local copies, waits for them, and re-layouts  14.5 us (4%)
  blocking collectives  6.91 us (2%)
  starting transfers between devices  5.21 us (1%)
    all_gather x1, waiting for transfers between devices, on_device(): lax.all_gather(down_weight, 'req', axis=1, tiled=True)  65.9 us
    all_gather x1, waiting for transfers between devices, on_device(): up_part = widen(lax.all_gather(up_weight, 'req', axis=0, tiled=True))  48.5 us
    all_gather x1, waiting for transfers between devices, on_device(): gate_part = widen(lax.all_gather(gate_weight, 'req', axis=0, tiled=True))  45.5 us
    all_gather x1, waiting for transfers between devices, on_device(): all_gather(partial_value.astype(jnp.bfloat16), 'hid')  26.1 us
    dot_general x1, matrix products, on_device(): jnp.dot(hidden, lax.all_gather(down_weight, 'req', axis=1, tiled=True), p...  20.9 us
    dot_general x1, matrix products, page_block(): jnp.einsum('pqhe,qheb->pheb', weights, page_terms, precision=TOP_PRECISION)  13.4 us
    dot_general x1, matrix products, page_block(): jnp.einsum('phik,phkv->phiv', raised_rows, previous, precision=TOP_PRECIS...  13.1 us
    dot_general x1, matrix products, widen(): return jnp.dot(feed_in, weight_rows, preferred_element_type=jnp.float32)  12 us
  transfers between devices with their start and end apart: 7, of which 5 were waited for; matrix products, arithmetic and copies ran while one was open for 20% of the time, Pallas kernels for 0%

profile of v1, /device:TPU:1, one launch (start us, length us, event | category | flops | bytes accessed | tf_op | source)
XLA Modules:
  0.0 386.6 jit_solution(4404167037331040253)
XLA Ops:
  10.8 7.3 %convolution_convert_fusion.2 = bf16[1024,1024]{1,0:T(8,128)(2,1)S(1)} fusion(bf16[2048,1024]{1,0:T(8,128)(2,1)} %param.20, bf16[1024,2048]{1,0:T(8,128)(2,1)S(1)} %copy-done.6, f32[2048]{0:T(1024)S(1)} %convert_element_type.151, f32[1024]{0:T(1024)S(1)} %add_rsqrt_fusion.2), kind=kOutput, calls=%fused_computation.53 | convolution fusion | flops 4304404480 | bytes 10498048 | tf_op jit(solution)/shard_map/dot_general | solution.py:144
  19.4 4.4 %collective-permute-start = (bf16[3,1024]{1,0:T(4,128)(2,1)S(1)}, bf16[3,1024]{1,0:T(4,128)(2,1)S(1)}, u32[]{:S(2)}, u32[]{:S(2)}) collective-permute-start(bf16[3,1024]{1,0:T(4,128)(2,1)S(1)} %slice_bitcast_fusion.5), channel_id=1, source_target_pairs={{0,2},{2,4},{4,6},{1,3},{3,5},{5,7},{8,10},{10,12},{12,14},{9,11},... | collective-permute-start | bytes 18440 | tf_op jit(solution)/shard_map/ppermute | solution.py:19
  24.0 5.2 %fusion.37 = f32[1024,256]{1,0:T(8,128)} fusion(bf16[16,256]{1,0:T(8,128)(2,1)S(1)} %copy-done.15, bf16[2048,16]{0,1:T(8,128)(2,1)S(1)} %copy-done.14, f32[256]{0:T(256)S(1)} %copy-done.16, bf16[1024,2048]{1,0:T(8,128)(2,1)} %param.18, f32[2048]{0:T(1024)S(1)} %convert_element_type.151, f32[1024]{0:T(1024)S(1)} %add_rsqrt_fusion.2), kind=kOutput, calls=%fused_computation.60 | convolution fusion | flops 86523904 | bytes 5329920 | tf_op jit(solution)/shard_map/dot_general | solution.py:157
  38.2 6.9 %all_gather.23 = bf16[4,1,256]{2,1,0:T(2,128)(2,1)S(1)} all-gather(bf16[1,1,256]{2,1,0:T(2,128)(2,1)S(1)} %fusion.71), channel_id=1, replica_groups=mesh['req'=16,'seq'=4,'hid'=2] {'seq'}, dimensions={0}, use_global_device_ids=true | all-gather | bytes 2560 | tf_op jit(solution)/shard_map/all_gather | solution.py:25
  45.2 7.6 %fusion.15 = f32[16,64,1,1024]{3,1,0,2:T(8,128)S(1)} fusion(f32[16,64,1024]{2,1,0:T(8,128)} %convert_element_type.154, f32[16,3,1024]{2,1,0:T(4,128)S(1)} %convert_multiply_fusion.4, f32[1024]{0:T(1024)S(1)} %bitcast.147, f32[1024]{0:T(1024)S(1)} %bitcast.148, f32[1024]{0:T(1024)S(1)} %bitcast.146, f32[1024]{0:T(1024)S(1)} %bitcast.145), kind=kLoop, calls=%fused_computation.29 | loop fusion | flops 10485760 | bytes 8601600 | tf_op jit(solution)/shard_map/reshape | solution.py:150
  52.9 7.4 %fusion.30 = f32[16,256,512]{2,1,0:T(8,128)S(1)} fusion(f32[16,64,1,1024]{3,1,0,2:T(8,128)S(1)} %fusion.15, f32[16,1,64,256]{3,0,1,2:T(8,128)S(1)} %fusion.48, f32[16,256]{1,0:T(8,128)S(1)} %get-tuple-element.85), kind=kOutput, calls=%fused_computation.51 | convolution fusion | flops 1612447744 | bytes 12599296 | tf_op jit(solution)/shard_map/phte,phtb->pheb/dot_general | solution.py:100
  60.3 13.4 %fusion.20 = f32[16,1,256,512]{3,0,2,1:T(8,128)S(1)} fusion(f32[16,256,512]{2,1,0:T(8,128)S(1)} %fusion.30, f32[16,256]{0,1:T(8,128)S(1)} %bitcast.142, pred[16,16]{1,0:T(8,128)(4,1)S(1)} %fusion.69), kind=kOutput, calls=%fused_computation.38 | convolution fusion | flops 402849792 | bytes 16793856 | tf_op jit(solution)/shard_map/pqhe,qheb->pheb/dot_general | solution.py:108
  78.7 4.2 %convolution_select_fusion = f32[16,64,64]{2,1,0:T(8,128)S(1)} fusion(f32[16,1,64,256]{3,0,1,2:T(8,128)S(1)} %fusion.48, pred[64,64]{1,0:T(8,128)(4,1)S(1)} %iota_compare_fusion, f32[16,64,1,1024]{3,1,0,2:T(8,128)} %copy-done.3), kind=kOutput, calls=%fused_computation.56 | convolution fusion | flops 204537856 | bytes 4464640 | tf_op jit(solution)/shard_map/phik,phjk->phij/dot_general | solution.py:93
  86.1 5.4 %multiply_bitcast_fusion = f32[16,256,512]{2,0,1:T(8,128)S(1)} fusion(f32[15,1,256,512]{3,0,2,1:T(8,128)} %bitcast.135, f32[16]{0:T(128)S(1)} %get-tuple-element.83), kind=kLoop, calls=%fused_computation.19 | loop fusion | flops 2097152 | bytes 16252992 | tf_op jit(solution)/shard_map/reshape.33
  91.5 13.1 %fusion.7 = f32[16,64,512]{2,1,0:T(8,128)} fusion(f32[16,256,512]{2,0,1:T(8,128)S(1)} %multiply_bitcast_fusion, f32[16,1,64,256]{3,0,1,2:T(8,128)S(1)} %fusion.48, f32[16,64,1,1024]{3,1,0,2:T(8,128)} %copy-done.3), kind=kOutput, calls=%fused_computation.14 | convolution fusion | flops 1611923456 | bytes 12582912 | tf_op jit(solution)/shard_map/phik,phkv->phiv/dot_general | solution.py:111
  104.6 6.8 %multiply_reduce_fusion = (f32[16,64]{1,0:T(8,128)S(1)}, f32[16,1,64,512]{3,2,0,1:T(8,128)}) fusion(f32[16,1,64,256]{3,0,1,2:T(8,128)} %copy-done.5, f32[16,256]{1,0:T(8,128)S(1)} %get-tuple-element.84, f32[16]{0:T(128)S(1)} %reduce.4, f32[16,64,1,1024]{3,1,0,2:T(8,128)} %copy-done.3, f32[1,256,512]{2,1,0:T(8,128)S(1)} %get-tuple-element.47, ...), kind=kOutput, calls=%fused_computation.46 | convolution fusion | flops 1614543872 | bytes 8933440 | tf_op jit(solution)/shard_map/dlof,lfg->dlog/dot_general | solution.py:183
  111.5 6.2 %fusion.25 = bf16[1024,512]{1,0:T(8,128)(2,1)S(1)} fusion(f32[16,1,64,512]{3,2,0,1:T(8,128)} %get-tuple-element.91, f32[512]{0:T(512)S(1)} %convert_element_type.165, f32[1024]{0:T(1024)S(1)} %rsqrt.29, bf16[2048,512]{1,0:T(8,128)(2,1)} %param.25, bf16[1024,2048]{1,0:T(8,128)(2,1)} %param.18, f32[2048]{0:T(1024)S(1)} %convert_element_type.151, ...), kind=kOutput, calls=%fused_computation.45 | convolution fusion | flops 2160066560 | bytes 9455616 | tf_op jit(solution)/shard_map/dot_general | solution.py:191
  117.7 4.4 %convolution_convert_fusion.1 = bf16[1024,2048]{1,0:T(8,128)(2,1)} fusion(bf16[1024,512]{1,0:T(8,128)(2,1)S(1)} %fusion.25, bf16[512,2048]{1,0:T(8,128)(2,1)S(1)} %copy-done), kind=kOutput, calls=%fused_computation.37 | convolution fusion | flops 2149580800 | bytes 7340032 | tf_op jit(solution)/shard_map/dot_general | solution.py:197
  124.2 26.1 %all-gather.15.cloned.1.call-done = bf16[2048,2048]{1,0:T(8,128)(2,1)} async-done(((bf16[1024,2048]{1,0:T(8,128)(2,1)}), bf16[2048,2048]{1,0:T(8,128)(2,1)}) %all-gather.15.cloned.1.call-update) | async-done | bytes 8388624 | tf_op jit(solution)/shard_map/all_gather | solution.py:200
  150.4 8.8 %reduce_sum.51 = bf16[1024,2048]{1,0:T(8,128)(2,1)} reduce(bf16[2,1024,2048]{2,1,0:T(8,128)(2,1)} %bitcast.137, bf16[]{:T(256)} %constant.84.clone.1), dimensions={0}, to_apply=%region_9.10 | reduce | flops 2097152 | bytes 12582914 | tf_op jit(solution)/shard_map/reduce_sum | solution.py:200
  159.2 7.5 %fusion = (f32[1024]{0:T(1024)S(1)}, bf16[1024,2048]{1,0:T(8,128)(2,1)}) fusion(bf16[1024,2048]{1,0:T(8,128)(2,1)} %reduce_sum.51, bf16[1024,2048]{1,0:T(8,128)(2,1)} %param.18), kind=kLoop, calls=%fused_computation.7 | loop fusion | flops 14679040 | bytes 12587008 | tf_op jit(solution)/shard_map/reduce_sum | solution.py:46
  166.7 45.5 %all-gather.9.cloned.1.call-done = bf16[2048,1408]{1,0:T(8,128)(2,1)} async-done(((bf16[128,1408]{1,0:T(8,128)(2,1)}), bf16[2048,1408]{1,0:T(8,128)(2,1)}) %all-gather.9.cloned.1.call-update) | async-done | bytes 5767184 | tf_op jit(solution)/shard_map/all_gather | solution.py:210
  212.2 12.0 %fusion.34 = f32[1024,1408]{1,0:T(8,128)} fusion(bf16[2048,1408]{1,0:T(8,128)(2,1)} %all-gather.9.cloned.1.call-done, bf16[1024,2048]{1,0:T(8,128)(2,1)} %get-tuple-element.81, f32[2048]{0:T(1024)S(1)} %convert_element_type.172, f32[1024]{0:T(1024)S(1)} %add_rsqrt_fusion.1), kind=kOutput, calls=%fused_computation.57 | convolution fusion | flops 5913968640 | bytes 15740928 | tf_op jit(solution)/shard_map/dot_general | solution.py:208
  224.2 48.5 %all-gather.11.cloned.1.call-done = bf16[2048,1408]{1,0:T(8,128)(2,1)} async-done(((bf16[128,1408]{1,0:T(8,128)(2,1)}), bf16[2048,1408]{1,0:T(8,128)(2,1)}) %all-gather.11.cloned.1.call-update) | async-done | bytes 5767184 | tf_op jit(solution)/shard_map/all_gather | solution.py:211
  272.7 65.9 %all-gather.13.cloned.1.call-done = bf16[1408,2048]{1,0:T(8,128)(2,1)} async-done(((bf16[1408,128]{1,0:T(8,128)(2,1)}), bf16[1408,2048]{1,0:T(8,128)(2,1)}) %all-gather.13.cloned.1.call-update) | async-done | bytes 5767184 | tf_op jit(solution)/shard_map/all_gather | solution.py:215
  338.6 20.9 %convolution_convert_fusion = bf16[1024,2048]{1,0:T(8,128)(2,1)} fusion(bf16[1408,2048]{1,0:T(8,128)(2,1)} %all-gather.13.cloned.1.call-done, f32[1024,1408]{1,0:T(8,128)} %fusion.34, bf16[2048,1408]{1,0:T(8,128)(2,1)} %all-gather.11.cloned.1.call-done, bf16[1024,2048]{1,0:T(8,128)(2,1)} %get-tuple-element.81, f32[2048]{0:T(1024)S(1)} %convert_element_type.172, ...), kind=kOutput, calls=%fused_computation.36 | convolution fusion | flops 11830296576 | bytes 25702400 | tf_op jit(solution)/shard_map/dot_general | solution.py:213
  365.4 4.5 %copy.71 = bf16[16,1,256,512]{3,2,1,0:T(8,128)(2,1)} copy(bf16[16,1,256,512]{3,0,2,1:T(8,128)(2,1)S(1)} %add_convert_fusion) | data formatting | bytes 8388608
  369.9 5.2 %reduce-scatter.2.cloned.1.call-done = bf16[512,2048]{1,0:T(8,128)(2,1)} async-done(((bf16[1024,2048]{1,0:T(8,128)(2,1)}), bf16[512,2048]{1,0:T(8,128)(2,1)}) %reduce-scatter.2.cloned.1.call-update) | async-done | bytes 2097168 | tf_op jit(solution)/shard_map/reduce_scatter | solution.py:218
  375.1 4.4 %add_convert_fusion.1 = bf16[512,2048]{1,0:T(8,128)(2,1)} fusion(bf16[512,2048]{1,0:T(8,128)(2,1)} %reduce-scatter.2.cloned.1.call-done, bf16[1024,2048]{1,0:T(8,128)(2,1)} %get-tuple-element.81, s32[]{:T(128)S(6)} %select_n.46), kind=kLoop, calls=%fused_computation.35 | loop fusion | flops 4194304 | bytes 6291460 | tf_op jit(solution)/shard_map/convert_element_type | solution.py:221
  (91 shorter events, 30.4 us)
Async XLA Ops:
  7.2 110.5 %copy-start = (bf16[512,2048]{1,0:T(8,128)(2,1)S(1)}, bf16[512,2048]{1,0:T(8,128)(2,1)}, u32[]{:S(2)}) copy-start(bf16[512,2048]{1,0:T(8,128)(2,1)} %param.27) | copy-start | bytes 6291460
  7.2 3.3 copy-start.9
  7.2 97.4 %all-gather.7.cloned.1.call-start = ((), (), s32[]{:S(2)}) async-start(), calls=%async_computation.1 | async-start | bytes 1310720 | tf_op jit(solution)/shard_map/all_gather | solution.py:25
  7.2 3.6 copy-start.6
  10.8 13.0 %copy-start.11 = (s32[1,16]{1,0:T(1,128)S(1)}, s32[1,16]{1,0:T(1,128)}, u32[]{:S(2)}) copy-start(s32[1,16]{1,0:T(1,128)} %param.33) | copy-start | bytes 196
  10.8 13.0 %copy-start.13 = (s32[1,16]{1,0:T(1,128)S(1)}, s32[1,16]{1,0:T(1,128)}, u32[]{:S(2)}) copy-start(s32[1,16]{1,0:T(1,128)} %param.32) | copy-start | bytes 196
  10.8 13.2 %copy-start.8 = (bf16[4,1024]{1,0:T(4,128)(2,1)S(1)}, bf16[4,1024]{1,0:T(4,128)(2,1)}, u32[]{:S(2)}) copy-start(bf16[4,1024]{1,0:T(4,128)(2,1)} %param.21) | copy-start | bytes 24580
  10.8 13.2 %copy-start.14 = (bf16[2048,16]{0,1:T(8,128)(2,1)S(1)}, bf16[2048,16]{0,1:T(8,128)(2,1)}, u32[]{:S(2)}) copy-start(bf16[2048,16]{0,1:T(8,128)(2,1)} %param.22) | copy-start | bytes 196612
  10.8 13.2 %copy-start.15 = (bf16[16,256]{1,0:T(8,128)(2,1)S(1)}, bf16[16,256]{1,0:T(8,128)(2,1)}, u32[]{:S(2)}) copy-start(bf16[16,256]{1,0:T(8,128)(2,1)} %param.23) | copy-start | bytes 24580
  10.8 13.2 %copy-start.16 = (f32[256]{0:T(256)S(1)}, f32[256]{0:T(256)}, u32[]{:S(2)}) copy-start(f32[256]{0:T(256)} %param.24) | copy-start | bytes 3076
  18.1 1.3 copy-start.7
  19.4 25.7 %collective-permute-start = (bf16[3,1024]{1,0:T(4,128)(2,1)S(1)}, bf16[3,1024]{1,0:T(4,128)(2,1)S(1)}, u32[]{:S(2)}, u32[]{:S(2)}) collective-permute-start(bf16[3,1024]{1,0:T(4,128)(2,1)S(1)} %slice_bitcast_fusion.5), channel_id=1, source_target_pairs={{0,2},{2,4},{4,6},{1,3},{3,5},{5,7},{8,10},{10,12},{12,14},{9,11},... | collective-permute-start | bytes 18440 | tf_op jit(solution)/shard_map/ppermute | solution.py:19
  29.2 9.0 %copy-start.12 = (bf16[512]{0:T(512)(128)(2,1)S(1)}, bf16[512]{0:T(512)(128)(2,1)}, u32[]{:S(2)}) copy-start(bf16[512]{0:T(512)(128)(2,1)} %param.26) | copy-start | bytes 3076
  31.0 60.4 %copy-start.5 = (f32[16,1,64,256]{3,0,1,2:T(8,128)}, f32[16,1,64,256]{3,0,1,2:T(8,128)S(1)}, u32[]{:S(2)}) copy-start(f32[16,1,64,256]{3,0,1,2:T(8,128)S(1)} %fusion.48) | copy-start | bytes 3145732
  52.9 7.4 %copy-start.3 = (f32[16,64,1,1024]{3,1,0,2:T(8,128)}, f32[16,64,1,1024]{3,1,0,2:T(8,128)S(1)}, u32[]{:S(2)}) copy-start(f32[16,64,1,1024]{3,1,0,2:T(8,128)S(1)} %fusion.15) | copy-start | bytes 12582916
  73.7 3.2 copy-start.2
  78.3 72.1 %all-gather.15.cloned.1.call-start = ((), (), s32[]{:S(2)}) async-start(), calls=%async_computation.6 | async-start | bytes 12582912 | tf_op jit(solution)/shard_map/all_gather | solution.py:200
  78.7 4.2 %copy-start.4 = (f32[16,64,1,1024]{3,1,0,2:T(8,128)S(1)}, f32[16,64,1,1024]{3,1,0,2:T(8,128)}, u32[]{:S(2)}) copy-start(f32[16,64,1,1024]{3,1,0,2:T(8,128)} %copy-done.3) | copy-start | bytes 12582916
  122.0 2.2 copy-start.10
  122.1 90.1 %all-gather.9.cloned.1.call-start = ((), (), s32[]{:S(2)}) async-start(), calls=%async_computation.2 | async-start | bytes 6127616 | tf_op jit(solution)/shard_map/all_gather | solution.py:210
  122.8 149.9 %all-gather.11.cloned.1.call-start = ((), (), s32[]{:S(2)}) async-start(), calls=%async_computation.3 | async-start | bytes 6127616 | tf_op jit(solution)/shard_map/all_gather | solution.py:211
  123.4 215.2 %all-gather.13.cloned.1.call-start = ((), (), s32[]{:S(2)}) async-start(), calls=%async_computation.4 | async-start | bytes 6127616 | tf_op jit(solution)/shard_map/all_gather | solution.py:215
  124.0 251.1 %reduce-scatter.2.cloned.1.call-start = ((), (), s32[]{:S(2)}) async-start(), calls=%async_computation.5 | async-start | bytes 6291456 | tf_op jit(solution)/shard_map/reduce_scatter | solution.py:218
  365.4 14.1 %copy-start.1 = (bf16[512,2048]{1,0:T(8,128)(2,1)S(1)}, bf16[512,2048]{1,0:T(8,128)(2,1)}, u32[]{:S(2)}) copy-start(bf16[512,2048]{1,0:T(8,128)(2,1)} %param.27) | copy-start | bytes 6291460
Sparse Core Ops, SparseCore 0:
  78.4 24.9 all-gather.6
  122.2 28.1 all-gather.14
  152.5 59.6 all-gather.8
  214.2 58.4 all-gather.10
  274.6 63.9 all-gather.12
  359.7 15.3 reduce-scatter.1
